TPU v7x, 128 devices: a whole 4x4x4 slice. The times are simulated.
128 devices in a mesh: grp: 8 (over y, x_lo), bal: 16 (over x_hi, z, core).
Axes of the slice: x: 4 (x_hi: 2, x_lo: 2; x = x_hi * 2 + x_lo), y: 4, z: 4, core: 2. Of those that a mesh axis runs over, the one named last changes fastest.
Arguments:
- events: bfloat16 [8, 8192, 512], P('grp', 'bal'), may hold values from -6 to 6
- cotangent: bfloat16 [8, 8192, 512], P('grp', 'bal'), may hold values from -6 to 6
- lengths: int32 [8, 16], P('grp'), may hold values from 1 to 16, as said below
- gain_in: float32 [512], replicated, may hold values from 0.1 to 1.9
- w_proj: bfloat16 [512, 2048], replicated, may hold values from -0.25 to 0.25
- gain_attn: float32 [512], replicated, may hold values from 0.1 to 1.9
- w_out: bfloat16 [512, 512], replicated, may hold values from -0.25 to 0.25
Outputs:
- d_x: bfloat16 [8, 8192, 512], P('grp', 'bal')
- grad_proj: float32 [512, 2048], replicated
- grad_out: float32 [512, 512], replicated
- grad_gain_in: float32 [512], replicated
- grad_gain_attn: float32 [512], replicated
Inputs may be any that keep to these rules, and one draw needn't show every extreme that they name: A group's 16 lengths count blocks of 64 events and sum to 128; in every group one length equals 16.
All inputs are finite; a program needn't handle non-finite values.
Results may differ from a plain program's by a relative error of at most 0.013.
Values may be sent and summed in bfloat16 or wider, within the bound.
No kernel may reach another device: no remote copies, remote signals or barrier semaphores. Data moves between devices by JAX's collectives and lax.ppermute only.
A program may use at most 256 MiB of HBM per device.

v0:
```python
import math
import jax
import jax.numpy as jnp
from jax import lax
from jax.sharding import PartitionSpec as P

HEADS = 8
BLOCK = 64
LEN_BLK = 16
epsilon = 1e-06


def norm_rows(values):
    mean_value = jnp.mean(values, axis=-1, keepdims=True)
    centred = values - mean_value
    rstd = lax.rsqrt(jnp.mean(centred * centred, axis=-1, keepdims=True) + epsilon)
    return (centred * rstd, rstd)


def silu_slope(values):
    sigma = jax.nn.sigmoid(values)
    return sigma * (1.0 + values * (1.0 - sigma))


def norm_back(grad, normed, rstd):
    return rstd * (
        grad
        - jnp.mean(grad, axis=-1, keepdims=True)
        - normed * jnp.mean(grad * normed, axis=-1, keepdims=True)
    )


def contract_rows(left, right):
    return lax.dot_general(
        left, right, (((0,), (0,)), ((), ())), preferred_element_type=jnp.float32
    )


def contract_cols(left, right):
    return lax.dot_general(
        left, right, (((1,), (1,)), ((), ())), preferred_element_type=jnp.float32
    )


def project_rows(rows, gain_in, w_proj):
    normed, rstd_in = norm_rows(rows.astype(jnp.float32))
    scaled = (normed * gain_in).astype(jnp.bfloat16)
    hidden = jnp.dot(scaled, w_proj, preferred_element_type=jnp.float32)
    active = jax.nn.silu(hidden).astype(jnp.bfloat16)
    return (normed, rstd_in, scaled, hidden, active)


def output_rows(attn, upper, grads_out, gain_attn, w_out):
    normed, rstd = norm_rows(attn.astype(jnp.float32))
    upper_wide = upper.astype(jnp.float32)
    mixed = (normed * gain_attn * upper_wide).astype(jnp.bfloat16)
    d_mixed = contract_cols(grads_out, w_out)
    d_upper = d_mixed * normed * gain_attn
    d_attn = norm_back(d_mixed * gain_attn * upper_wide, normed, rstd).astype(jnp.bfloat16)
    out_term = contract_rows(mixed, grads_out)
    gain_term = jnp.sum(d_mixed * normed * upper_wide, axis=0)
    return (d_upper, d_attn, out_term, gain_term)


def input_rows(grads_out, d_act, hidden, normed, rstd_in, scaled, gain_in, w_proj):
    d_hidden = (d_act * silu_slope(hidden)).astype(jnp.bfloat16)
    proj_term = contract_rows(scaled, d_hidden)
    d_scaled = contract_cols(d_hidden, w_proj)
    d_rows = (
        grads_out.astype(jnp.float32) + norm_back(d_scaled * gain_in, normed, rstd_in)
    ).astype(jnp.bfloat16)
    gain_term = jnp.sum(d_scaled * normed, axis=0)
    return (d_rows, proj_term, gain_term)


def attend_forward(query, keys, values, allowed):
    head_width = query.shape[1] // HEADS
    scale = head_width ** (-0.5)
    outputs = []
    for head in range(HEADS):
        columns = slice(head * head_width, (head + 1) * head_width)
        scores = contract_cols(query[:, columns], keys[:, columns]) * scale
        weights = (jax.nn.silu(scores) * allowed).astype(jnp.bfloat16)
        outputs.append(jnp.dot(weights, values[:, columns], preferred_element_type=jnp.float32))
    return jnp.concatenate(outputs, axis=1).astype(jnp.bfloat16)


def attend_backward(query, keys, values, grad_attn, allowed):
    head_width = query.shape[1] // HEADS
    scale = head_width ** (-0.5)
    grads_query, grads_keys, grads_values = ([], [], [])
    for head in range(HEADS):
        columns = slice(head * head_width, (head + 1) * head_width)
        query_head = query[:, columns]
        key_head = keys[:, columns]
        grad_head = grad_attn[:, columns]
        scores = contract_cols(query_head, key_head) * scale
        weights = (jax.nn.silu(scores) * allowed).astype(jnp.bfloat16)
        grad_weights = contract_cols(grad_head, values[:, columns])
        grad_scores = (grad_weights * silu_slope(scores) * allowed).astype(jnp.bfloat16)
        grads_values.append(contract_rows(weights, grad_head).astype(jnp.bfloat16))
        grads_query.append(
            (jnp.dot(grad_scores, key_head, preferred_element_type=jnp.float32) * scale).astype(
                jnp.bfloat16
            )
        )
        grads_keys.append((contract_rows(grad_scores, query_head) * scale).astype(jnp.bfloat16))
    return (
        jnp.concatenate(grads_query, axis=1),
        jnp.concatenate(grads_keys, axis=1),
        jnp.concatenate(grads_values, axis=1),
    )


def lookup(table, positions):
    entries = jnp.arange(table.shape[0], dtype=jnp.int32)
    picked = jnp.where(entries[None, :] == positions[:, None], table[None, :], 0)
    return jnp.sum(picked, axis=1)


def regroup(table, rows):
    blocks = rows.reshape(table.shape[1], -1)
    moved = jnp.dot(table, blocks, preferred_element_type=jnp.float32)
    return moved.astype(jnp.bfloat16).reshape(-1, rows.shape[1])


def pack_histories(seq_lengths):

    def advance(state, length_now):
        device_rank, held_blocks = state
        fresh = held_blocks + length_now > LEN_BLK
        device_rank = device_rank + fresh.astype(jnp.int32)
        held_blocks = jnp.where(fresh, 0, held_blocks) + length_now
        return ((device_rank, held_blocks), device_rank)

    start_state = (jnp.int32(0), jnp.int32(0))
    final_state, ranks = lax.scan(advance, start_state, seq_lengths)
    return ranks


def held_tiles_map(tile_fn, live_tiles, inputs, tile_rows):
    count = inputs[0].shape[0] // tile_rows
    pieces = tuple((array.reshape((count, tile_rows) + array.shape[1:]) for array in inputs))

    def blank_fn(parts):
        return jax.tree.map(jnp.zeros_like, tile_fn(parts))

    def each_tile(item):
        position, parts = item
        return lax.cond(position < live_tiles, tile_fn, blank_fn, parts)

    return lax.map(each_tile, (jnp.arange(count, dtype=jnp.int32), pieces))


def flatten_tiles(array):
    return array.reshape((-1,) + array.shape[2:])


def whole_layer(rows, grads_out, allowed, live_tiles, tile_rows, gain_in, w_proj, gain_attn, w_out):
    width = rows.shape[1]
    first = held_tiles_map(
        lambda parts: project_rows(parts[0], gain_in, w_proj), live_tiles, (rows,), tile_rows
    )
    normed, rstd_in, scaled, hidden, active = jax.tree.map(flatten_tiles, first)
    upper = active[:, :width]
    values = active[:, width : 2 * width]
    query = active[:, 2 * width : 3 * width]
    keys = active[:, 3 * width :]
    attn = attend_forward(query, keys, values, allowed)
    second = held_tiles_map(
        lambda parts: output_rows(parts[0], parts[1], parts[2], gain_attn, w_out),
        live_tiles,
        (attn, upper, grads_out),
        tile_rows,
    )
    d_upper = flatten_tiles(second[0])
    d_attn = flatten_tiles(second[1])
    out_term = jnp.sum(second[2], axis=0)
    gain_attn_term = jnp.sum(second[3], axis=0)
    d_query, d_keys, d_values = attend_backward(query, keys, values, d_attn, allowed)
    d_act = jnp.concatenate(
        [
            d_upper,
            d_values.astype(jnp.float32),
            d_query.astype(jnp.float32),
            d_keys.astype(jnp.float32),
        ],
        axis=1,
    )
    third = held_tiles_map(
        lambda parts: input_rows(
            parts[0], parts[1], parts[2], parts[3], parts[4], parts[5], gain_in, w_proj
        ),
        live_tiles,
        (grads_out, d_act, hidden, normed, rstd_in, scaled),
        tile_rows,
    )
    d_rows = flatten_tiles(third[0])
    proj_term = jnp.sum(third[1], axis=0)
    gain_in_term = jnp.sum(third[2], axis=0)
    return (d_rows, (proj_term, out_term, gain_in_term, gain_attn_term))


def per_device(events, cotangent, lengths, gain_in, w_proj, gain_attn, w_out):
    peers = lax.axis_size("bal")
    own_index = lax.axis_index("bal")
    local_rows = events[0]
    local_grads = cotangent[0]
    local_blocks = local_rows.shape[0] // BLOCK
    slots = LEN_BLK // peers
    seq_lengths = lengths[0]
    targets = pack_histories(seq_lengths)
    ends = jnp.cumsum(seq_lengths)
    device_ids = jnp.arange(peers, dtype=jnp.int32)
    range_starts = jnp.sum(
        jnp.where(targets[None, :] < device_ids[:, None], seq_lengths[None, :], 0), axis=1
    )
    range_sizes = jnp.sum(
        jnp.where(targets[None, :] == device_ids[:, None], seq_lengths[None, :], 0), axis=1
    )
    flat_blocks = own_index + peers * jnp.arange(local_blocks, dtype=jnp.int32)
    owner_seq = jnp.sum((ends[None, :] <= flat_blocks[:, None]).astype(jnp.int32), axis=1)
    owner = lookup(targets, owner_seq)
    slot_index = (flat_blocks - lookup(range_starts, owner)) // peers
    slot_ids = jnp.arange(peers * slots, dtype=jnp.int32)
    send_table = (slot_ids[:, None] == (owner * slots + slot_index)[None, :]).astype(jnp.bfloat16)
    mine_start = lookup(range_starts, own_index[None])[0]
    mine_size = lookup(range_sizes, own_index[None])[0]
    block_order = jnp.arange(LEN_BLK, dtype=jnp.int32)
    from_slot = (mine_start + block_order) % peers * slots + block_order // peers
    take_table = (from_slot[:, None] == slot_ids[None, :]).astype(jnp.bfloat16)
    return_table = jnp.transpose(take_table)
    home_table = jnp.transpose(send_table)
    block_seq = jnp.sum(
        (ends[None, :] <= (mine_start + block_order)[:, None]).astype(jnp.int32), axis=1
    )
    block_seq = jnp.where(block_order < mine_size, block_seq, -1)
    row_seq = jnp.repeat(block_seq, BLOCK)
    positions = jnp.arange(LEN_BLK * BLOCK, dtype=jnp.int32)
    allowed = (
        (row_seq[:, None] == row_seq[None, :])
        & (row_seq[:, None] >= 0)
        & (positions[None, :] <= positions[:, None])
    ).astype(jnp.float32)
    tile_blocks = math.gcd(LEN_BLK, max(1, 256 // BLOCK))
    live_tiles = (mine_size + tile_blocks - 1) // tile_blocks
    got_rows, got_grads = (
        lax.all_to_all(
            regroup(send_table, local_rows), "bal", split_axis=0, concat_axis=0, tiled=True
        ),
        lax.all_to_all(
            regroup(send_table, local_grads), "bal", split_axis=0, concat_axis=0, tiled=True
        ),
    )
    held_rows = regroup(take_table, got_rows)
    held_grads = regroup(take_table, got_grads)
    d_held, terms = whole_layer(
        held_rows,
        held_grads,
        allowed,
        live_tiles,
        tile_blocks * BLOCK,
        gain_in,
        w_proj,
        gain_attn,
        w_out,
    )
    came_back = lax.all_to_all(
        regroup(return_table, d_held), "bal", split_axis=0, concat_axis=0, tiled=True
    )
    d_rows = regroup(home_table, came_back)
    sums = lax.psum((terms[0], terms[1], terms[2], terms[3]), ("grp", "bal"))
    divisor = float(lax.axis_size("grp") * peers)
    return (
        d_rows[None],
        sums[0] / divisor,
        sums[1] / divisor,
        sums[2] / divisor,
        sums[3] / divisor,
    )


def solution(mesh):
    placed = (P("grp", "bal", None), P("grp", "bal", None), P("grp", None), P(), P(), P(), P())
    return jax.shard_map(
        per_device,
        mesh=mesh,
        in_specs=placed,
        out_specs=(P("grp", "bal", None), P(), P(), P(), P()),
        check_vma=False,
    )
```

profile of v0, /device:TPU:1, one launch (start us, length us, event | category | flops | bytes accessed | tf_op | source)
XLA Modules:
  0.0 636.9 jit_solution(15162623421532527161)
XLA Ops:
  7.2 42.6 %while.66 = (s32[]{:T(128)}, s32[]{:T(128)}, s32[]{:T(128)}, s32[16]{0:T(128)S(1)}, s32[16]{0:T(128)}) while((s32[]{:T(128)}, s32[]{:T(128)}, s32[]{:T(128)}, s32[16]{0:T(128)S(1)}, s32[16]{0:T(128)}) %tuple.198), condition=%wide.region_3.4_spmd.clone, body=%wide.region_2.3_spmd.sunk.clone | while | flops 8 | bytes 148 | solution.py:137
  55.1 9.3 %all-to-all-start.1 = ((bf16[16,64,512]{2,1,0:T(8,128)(2,1)}), bf16[16,64,512]{2,1,0:T(8,128)(2,1)S(1)}, u32[]{:S(2)}, u32[]{:S(2)}) async-start(bf16[16,64,512]{2,1,0:T(8,128)(2,1)} %bitcast.70), calls=%async_computation.1 | async-start | bytes 2097152 | tf_op jit(solution)/shard_map/all_to_all | solution.py:248
  70.0 11.6 %all-to-all-done.1 = bf16[16,64,512]{2,1,0:T(8,128)(2,1)S(1)} async-done(((bf16[16,64,512]{2,1,0:T(8,128)(2,1)}), bf16[16,64,512]{2,1,0:T(8,128)(2,1)S(1)}, u32[]{:S(2)}, u32[]{:S(2)}) %all-to-all-start.1) | async-done | bytes 1048608 | tf_op jit(solution)/shard_map/all_to_all | solution.py:248
  81.6 5.0 all-to-all-start
  91.9 70.2 %while.67 = (s32[]{:T(128)}, f32[4,256,512]{2,1,0:T(8,128)}, f32[4,256,1]{1,2,0:T(1,128)}, bf16[4,256,512]{2,1,0:T(8,128)(2,1)}, f32[4,256,2048]{2,1,0:T(8,128)}...) while((s32[]{:T(128)}, f32[4,256,512]{2,1,0:T(8,128)}, ...), condition=%wide.region_16.17_spmd.clone, body=%wide.region_11.16_spmd.sunk.clone | while | flops 541589760 | bytes 17060060 | solution.py:152
  93.2 9.2 %conditional.9 = (f32[1,256,512]{2,1,0:T(8,128)S(1)}, f32[1,256,1]{1,2,0:T(1,128)}, bf16[1,256,512]{2,1,0:T(8,128)(2,1)S(1)}, f32[1,256,2048]{2,1,0:T(8,128)}, bf16[1,256,2048]{2,1,0:T(8,128)(2,1)S(1)}) conditional(s32[]{:T(128)} %convert_element_type.475, () %tuple.157, (bf16[4,256,512]{2,1,0:T(8,128)(2,1)}, s32[]{:T(128)}, f32[512]{0:T(512)S(1)}, ...), branch_computations={%region_12.12_spmd, %region_13.15_spmd} | conditional | flops 541589760 | bytes 9190964 | solution.py:150
  110.8 9.2 %conditional.9 = (f32[1,256,512]{2,1,0:T(8,128)S(1)}, f32[1,256,1]{1,2,0:T(1,128)}, bf16[1,256,512]{2,1,0:T(8,128)(2,1)S(1)}, f32[1,256,2048]{2,1,0:T(8,128)}, bf16[1,256,2048]{2,1,0:T(8,128)(2,1)S(1)}) conditional(s32[]{:T(128)} %convert_element_type.475, () %tuple.157, (bf16[4,256,512]{2,1,0:T(8,128)(2,1)}, s32[]{:T(128)}, f32[512]{0:T(512)S(1)}, ...), branch_computations={%region_12.12_spmd, %region_13.15_spmd} | conditional | flops 541589760 | bytes 9190964 | solution.py:150
  128.4 9.2 %conditional.9 = (f32[1,256,512]{2,1,0:T(8,128)S(1)}, f32[1,256,1]{1,2,0:T(1,128)}, bf16[1,256,512]{2,1,0:T(8,128)(2,1)S(1)}, f32[1,256,2048]{2,1,0:T(8,128)}, bf16[1,256,2048]{2,1,0:T(8,128)(2,1)S(1)}) conditional(s32[]{:T(128)} %convert_element_type.475, () %tuple.157, (bf16[4,256,512]{2,1,0:T(8,128)(2,1)}, s32[]{:T(128)}, f32[512]{0:T(512)S(1)}, ...), branch_computations={%region_12.12_spmd, %region_13.15_spmd} | conditional | flops 541589760 | bytes 9190964 | solution.py:150
  145.9 9.2 %conditional.9 = (f32[1,256,512]{2,1,0:T(8,128)S(1)}, f32[1,256,1]{1,2,0:T(1,128)}, bf16[1,256,512]{2,1,0:T(8,128)(2,1)S(1)}, f32[1,256,2048]{2,1,0:T(8,128)}, bf16[1,256,2048]{2,1,0:T(8,128)(2,1)S(1)}) conditional(s32[]{:T(128)} %convert_element_type.475, () %tuple.157, (bf16[4,256,512]{2,1,0:T(8,128)(2,1)}, s32[]{:T(128)}, f32[512]{0:T(512)S(1)}, ...), branch_computations={%region_12.12_spmd, %region_13.15_spmd} | conditional | flops 541589760 | bytes 9190964 | solution.py:150
  186.4 19.1 %select_convert_fusion.8 = (bf16[1024,1024]{1,0:T(8,128)(2,1)S(1)}, bf16[1024,1024]{1,0:T(8,128)(2,1)}, bf16[1024,1024]{1,0:T(8,128)(2,1)}, bf16[1024,1024]{1,0:...) fusion(pred[1024]{0:T(1024)(128)(4,1)S(1)} %broadcast_compare_f, ...), kind=kOutput, calls=%fused_computation.122 | convolution fusion | flops 197132288 | bytes 50865152 | tf_op jit(solution)/shard_map/dot_general | solution.py:40
  237.3 35.1 %while.68 = (s32[]{:T(128)}, f32[4,256,512]{2,1,0:T(8,128)}, bf16[4,256,512]{2,1,0:T(8,128)(2,1)}, f32[4,512,512]{2,1,0:T(8,128)}, f32[4,512]{1,0:T(4,128)S(1)},...) while((s32[]{:T(128)}, f32[4,256,512]{2,1,0:T(8,128)}, ...), condition=%wide.region_25.26_spmd.clone, body=%wide.region_17.25_spmd.sunk.clone | while | flops 273415936 | bytes 9736943 | solution.py:152
  238.5 4.9 conditional.10
  282.7 5.2 select_convert_fusion.1
  288.0 4.9 select_convert_fusion.2
  297.7 4.9 select_convert_fusion.4
  307.4 4.9 select_convert_fusion.6
  317.2 4.9 select_convert_fusion
  372.0 5.6 pad_maximum_fusion
  377.8 67.9 %while.69 = (s32[]{:T(128)}, bf16[4,256,512]{2,1,0:T(8,128)(2,1)S(1)}, f32[4,512,2048]{2,1,0:T(8,128)}, f32[4,512]{1,0:T(4,128)S(1)}, s32[4]{0:T(128)S(1)}, /*in...) while((s32[]{:T(128)}, ...), condition=%wide.region_32.33_spmd.clone, body=%wide.region_26.32_spmd.sunk.clone | while | flops 1085013504 | bytes 26500880 | solution.py:152
  379.3 10.9 %conditional.11 = (bf16[1,256,512]{2,1,0:T(8,128)(2,1)S(1)}, f32[1,512,2048]{2,1,0:T(8,128)}, f32[1,512]{1,0:T(1,128)S(1)}) conditional(s32[]{:T(128)} %convert_element_type.477, () %tuple.167, (bf16[4,256,512]{2,1,0:T(8,128)(2,1)}, s32[]{:T(128)}, f32[4,256,1]{1,2,0:T(1,128)}, f32[4,256,2048]{2,1,0:T(8,128)}, f32[4,256,2048]{2,1,0:T(8,128)}, ...), branch_computations={%region_27.27_spmd, %region_28.31_spmd} | conditional | flops 1085013504 | bytes 17583136 | solution.py:150
  384.7 5.5 convolution_bitcast_fusion.1
  396.1 10.9 %conditional.11 = (bf16[1,256,512]{2,1,0:T(8,128)(2,1)S(1)}, f32[1,512,2048]{2,1,0:T(8,128)}, f32[1,512]{1,0:T(1,128)S(1)}) conditional(s32[]{:T(128)} %convert_element_type.477, () %tuple.167, (bf16[4,256,512]{2,1,0:T(8,128)(2,1)}, s32[]{:T(128)}, f32[4,256,1]{1,2,0:T(1,128)}, f32[4,256,2048]{2,1,0:T(8,128)}, f32[4,256,2048]{2,1,0:T(8,128)}, ...), branch_computations={%region_27.27_spmd, %region_28.31_spmd} | conditional | flops 1085013504 | bytes 17583136 | solution.py:150
  401.6 5.5 convolution_bitcast_fusion.1
  413.1 11.0 %conditional.11 = (bf16[1,256,512]{2,1,0:T(8,128)(2,1)S(1)}, f32[1,512,2048]{2,1,0:T(8,128)}, f32[1,512]{1,0:T(1,128)S(1)}) conditional(s32[]{:T(128)} %convert_element_type.477, () %tuple.167, (bf16[4,256,512]{2,1,0:T(8,128)(2,1)}, s32[]{:T(128)}, f32[4,256,1]{1,2,0:T(1,128)}, f32[4,256,2048]{2,1,0:T(8,128)}, f32[4,256,2048]{2,1,0:T(8,128)}, ...), branch_computations={%region_27.27_spmd, %region_28.31_spmd} | conditional | flops 1085013504 | bytes 17583136 | solution.py:150
  418.5 5.5 convolution_bitcast_fusion.1
  430.0 11.0 %conditional.11 = (bf16[1,256,512]{2,1,0:T(8,128)(2,1)S(1)}, f32[1,512,2048]{2,1,0:T(8,128)}, f32[1,512]{1,0:T(1,128)S(1)}) conditional(s32[]{:T(128)} %convert_element_type.477, () %tuple.167, (bf16[4,256,512]{2,1,0:T(8,128)(2,1)}, s32[]{:T(128)}, f32[4,256,1]{1,2,0:T(1,128)}, f32[4,256,2048]{2,1,0:T(8,128)}, f32[4,256,2048]{2,1,0:T(8,128)}, ...), branch_computations={%region_27.27_spmd, %region_28.31_spmd} | conditional | flops 1085013504 | bytes 17583136 | solution.py:150
  435.5 5.5 convolution_bitcast_fusion.1
  445.7 10.1 %reduce_sum.224 = f32[512,2048]{1,0:T(8,128)} reduce(f32[4,512,2048]{2,1,0:T(8,128)} %get-tuple-element.445, f32[]{:T(128)} %constant.270.clone.1), dimensions={0}, to_apply=%region_33.34 | reduce | flops 3145728 | bytes 20971524 | tf_op jit(solution)/shard_map/reduce_sum | solution.py:199
  462.0 5.8 all-to-all-start.2
  467.8 73.7 %all-reduce = (f32[512]{0:T(512)S(1)}, f32[512]{0:T(512)S(1)}) all-reduce(f32[512]{0:T(512)S(1)} %reduce_sum.226, f32[512]{0:T(512)S(1)} %reduce_sum.227), channel_id=1, replica_groups=mesh['grp'=8,'bal'=16] {'grp','bal'}, use_global_device_ids=true, to_apply=%region_38.39 | all-reduce | flops 1024 | bytes 8192 | tf_op jit(solution)/shard_map/psum | solution.py:272
  544.6 79.3 %all-reduce.4.cloned.1.call-done = (f32[512,2048]{1,0:T(8,128)}, f32[512,512]{1,0:T(8,128)}) async-done(((f32[512,2048]{1,0:T(8,128)}, f32[512,512]{1,0:T(8,128)}), (f32[512,2048]{1,0:T(8,128)}, f32[512,512]{1,0:T(8,128)})) %all-reduce.4.cloned.1.call-update) | async-done | bytes 5242896 | tf_op jit(solution)/shard_map/psum | solution.py:272
  623.9 4.9 broadcast_multiply_fusion.6
  (404 shorter events, 334.8 us)
Async XLA Ops:
  7.2 60.8 %copy-start.36 = (bf16[1,512,512]{2,1,0:T(8,128)(2,1)S(1)}, bf16[1,512,512]{2,1,0:T(8,128)(2,1)}, u32[]{:S(2)}) copy-start(bf16[1,512,512]{2,1,0:T(8,128)(2,1)} %param.22) | copy-start | bytes 1572868
  52.0 16.6 %copy-start.40 = (s32[8]{0:T(128)}, s32[8]{0:T(128)S(1)}, u32[]{:S(2)}) copy-start(s32[8]{0:T(128)S(1)} %fusion.169) | copy-start | bytes 100
  55.1 26.5 %all-to-all-start.1 = ((bf16[16,64,512]{2,1,0:T(8,128)(2,1)}), bf16[16,64,512]{2,1,0:T(8,128)(2,1)S(1)}, u32[]{:S(2)}, u32[]{:S(2)}) async-start(bf16[16,64,512]{2,1,0:T(8,128)(2,1)} %bitcast.70), calls=%async_computation.1 | async-start | bytes 2097152 | tf_op jit(solution)/shard_map/all_to_all | solution.py:248
  67.0 163.3 %copy-start.42 = (s32[16]{0:T(128)}, s32[16]{0:T(128)S(1)}, u32[]{:S(2)}) copy-start(s32[16]{0:T(128)S(1)} %get-tuple-element.578) | copy-start | bytes 196
  81.6 147.0 %all-to-all-start = ((bf16[16,64,512]{2,1,0:T(8,128)(2,1)}), bf16[16,64,512]{2,1,0:T(8,128)(2,1)}, u32[]{:S(2)}, u32[]{:S(2)}) async-start(bf16[16,64,512]{2,1,0:T(8,128)(2,1)} %bitcast.66), calls=%async_computation | async-start | bytes 2097152 | tf_op jit(solution)/shard_map/all_to_all | solution.py:251
  86.6 537.4 %all-reduce.4.cloned.1.call-start = ((), (), s32[]{:S(2)}) async-start(), calls=%async_computation.3 | async-start | bytes 10485760 | tf_op jit(solution)/shard_map/psum | solution.py:272
  186.4 19.1 %copy-start.15 = (f32[1024,1024]{1,0:T(8,128)}, f32[1024,1024]{1,0:T(8,128)S(1)}, u32[]{:S(2)}) copy-start(f32[1024,1024]{1,0:T(8,128)S(1)} %fusion.155) | copy-start | bytes 12582916
  205.5 7.7 %copy-start.8 = (bf16[1024,1024]{1,0:T(8,128)(2,1)}, bf16[1024,1024]{1,0:T(8,128)(2,1)S(1)}, u32[]{:S(2)}) copy-start(bf16[1024,1024]{1,0:T(8,128)(2,1)S(1)} %get-tuple-element.573) | copy-start | bytes 6291460
  205.5 7.7 %copy-start.10 = (bf16[1024,1024]{1,0:T(8,128)(2,1)}, bf16[1024,1024]{1,0:T(8,128)(2,1)S(1)}, u32[]{:S(2)}) copy-start(bf16[1024,1024]{1,0:T(8,128)(2,1)S(1)} %get-tuple-element.574) | copy-start | bytes 6291460
  205.5 7.7 %copy-start.6 = (bf16[1024,1024]{1,0:T(8,128)(2,1)}, bf16[1024,1024]{1,0:T(8,128)(2,1)S(1)}, u32[]{:S(2)}) copy-start(bf16[1024,1024]{1,0:T(8,128)(2,1)S(1)} %get-tuple-element.572) | copy-start | bytes 6291460
  205.5 9.4 %copy-start.12 = (bf16[1024,1024]{1,0:T(8,128)(2,1)}, bf16[1024,1024]{1,0:T(8,128)(2,1)S(1)}, u32[]{:S(2)}) copy-start(bf16[1024,1024]{1,0:T(8,128)(2,1)S(1)} %get-tuple-element.575) | copy-start | bytes 6291460
  205.5 9.4 %copy-start.13 = (bf16[1024,1024]{1,0:T(8,128)(2,1)}, bf16[1024,1024]{1,0:T(8,128)(2,1)S(1)}, u32[]{:S(2)}) copy-start(bf16[1024,1024]{1,0:T(8,128)(2,1)S(1)} %get-tuple-element.569) | copy-start | bytes 6291460
  205.5 20.4 %copy-start.2 = (bf16[1024,1024]{1,0:T(8,128)(2,1)}, bf16[1024,1024]{1,0:T(8,128)(2,1)S(1)}, u32[]{:S(2)}) copy-start(bf16[1024,1024]{1,0:T(8,128)(2,1)S(1)} %get-tuple-element.576) | copy-start | bytes 6291460
  230.8 6.4 %copy-start.37 = (f32[512]{0:T(512)S(1)}, f32[512]{0:T(512)}, u32[]{:S(2)}) copy-start(f32[512]{0:T(512)} %param.26) | copy-start | bytes 6148
  272.4 5.3 copy-start.38
  282.7 5.2 copy-start.21
  288.0 4.9 copy-start.20
  292.9 4.8 copy-start.19
  297.7 4.9 copy-start.18
  302.6 4.8 copy-start.17
  307.4 4.9 copy-start.16
  312.3 4.8 copy-start.44
  359.1 4.9 copy-start.32
  359.1 5.1 copy-start.33
  359.1 5.2 copy-start.34
  359.1 5.4 copy-start.35
  372.0 5.8 copy-start.1
  372.0 5.8 copy-start.31
  459.6 8.2 %copy-start.39 = (f32[4,512]{1,0:T(4,128)S(1)}, f32[4,512]{1,0:T(4,128)}, u32[]{:S(2)}) copy-start(f32[4,512]{1,0:T(4,128)} %copy-done.38) | copy-start | bytes 24580
  460.2 83.1 %copy-start.41 = (s32[8]{0:T(128)S(1)}, s32[8]{0:T(128)}, u32[]{:S(2)}) copy-start(s32[8]{0:T(128)} %copy-done.40) | copy-start | bytes 100
  462.0 80.6 %all-to-all-start.2 = ((bf16[16,64,512]{2,1,0:T(8,128)(2,1)}), bf16[16,64,512]{2,1,0:T(8,128)(2,1)S(1)}, u32[]{:S(2)}, u32[]{:S(2)}) async-start(bf16[16,64,512]{2,1,0:T(8,128)(2,1)} %bitcast.74), calls=%async_computation.2 | async-start | bytes 2097152 | tf_op jit(solution)/shard_map/all_to_all | solution.py:268
  623.9 4.9 copy-start.25
  (17 other events, 48.2 us)
Sparse Core Ops, SparseCore 0:
  459.7 164.1 all-reduce.3
where the time goes:
time: 644 us; the launch traced here: 637 us
  matrix products  205 us (32%)
  local copies, waits for them, and re-layouts  132 us (20%)
  waiting for transfers between devices  90.9 us (14%)
  blocking collectives  73.7 us (11%)
  other arithmetic  70.4 us (11%)
  loops' own time  29.7 us (5%)
  starting transfers between devices  20.1 us (3%)
  between operations  16 us (2%)
    dot_general x24, matrix products, contract_cols(): lax.dot_general(left, right, (((1,), (1,)), ((), ())), preferred_element_...  103 us
    psum x1, waiting for transfers between devices, per_device(): sums = lax.psum((terms[0], terms[1], terms[2], terms[3]), ('grp', 'bal'))  79.3 us
    psum x1, blocking collectives, per_device(): sums = lax.psum((terms[0], terms[1], terms[2], terms[3]), ('grp', 'bal'))  73.7 us
    dynamic_update_slice x48, local copies, waits for them, and re-layouts, held_tiles_map(): return lax.map(each_tile, (jnp.arange(count, dtype=jnp.int32), pieces))  57.7 us
    dot_general x24, matrix products, contract_rows(): lax.dot_general(left, right, (((0,), (0,)), ((), ())), preferred_element_...  51.2 us
    another operation x1, loops' own time, pack_histories(): final_state, ranks = lax.scan(advance, start_state, seq_lengths)  20.9 us
    dynamic_slice x16, local copies, waits for them, and re-layouts, pack_histories(): final_state, ranks = lax.scan(advance, start_state, seq_lengths)  19.9 us
    dot_general x8, matrix products, attend_backward(): jnp.dot(grad_scores, key_head, preferred_element_type=jnp.float32) * scale  19.2 us
  transfers between devices with their start and end apart: 4, of which 2 were waited for; matrix products, arithmetic and copies ran while one was open for 23% of the time, Pallas kernels for 0%

commit v1 on v0

--- a/solution.py
+++ b/solution.py
@@ -269,7 +269,8 @@
         regroup(return_table, d_held), "bal", split_axis=0, concat_axis=0, tiled=True
     )
     d_rows = regroup(home_table, came_back)
-    sums = lax.psum((terms[0], terms[1], terms[2], terms[3]), ("grp", "bal"))
+    one_axis = lax.psum((terms[0], terms[1], terms[2], terms[3]), "grp")
+    sums = lax.psum(one_axis, "bal")
     divisor = float(lax.axis_size("grp") * peers)
     return (
         d_rows[None],

time: 644 us -> 864 us (1.34)
  waiting for transfers between devices: 90.9 us -> 320 us
  blocking collectives: 73.7 us -> 63.3 us
    psum x1 -> x2, waiting for transfers between devices: 79.3 us -> 308 us  [the longest x1 222 us: per_device(): one_axis = lax.psum((terms[0], terms[1], terms[2], terms[3]), 'grp')]
    psum x1 -> x2, blocking collectives: 73.7 us -> 63.3 us  [the longest x1 35.5 us: per_device(): sums = lax.psum(one_axis, 'bal')]
  transfers between devices with their start and end apart: 4 -> 5, of which waited for: 2 -> 3; matrix products, arithmetic and copies ran while one was open for 23% -> 17% of each run, Pallas kernels for 0% -> 0%
where the time goes in v1:
time: 864 us; the launch traced here: 857 us
  waiting for transfers between devices  320 us (37%)
  matrix products  205 us (24%)
  local copies, waits for them, and re-layouts  132 us (15%)
  other arithmetic  70.4 us (8%)
  blocking collectives  63.3 us (7%)
  loops' own time  29.7 us (3%)
  starting transfers between devices  21.8 us (3%)
  between operations  16.1 us (2%)
    psum x1, waiting for transfers between devices, per_device(): one_axis = lax.psum((terms[0], terms[1], terms[2], terms[3]), 'grp')  222 us
    dot_general x24, matrix products, contract_cols(): lax.dot_general(left, right, (((1,), (1,)), ((), ())), preferred_element_...  103 us
    psum x1, waiting for transfers between devices, per_device(): sums = lax.psum(one_axis, 'bal')  86.2 us
    dynamic_update_slice x48, local copies, waits for them, and re-layouts, held_tiles_map(): return lax.map(each_tile, (jnp.arange(count, dtype=jnp.int32), pieces))  57.7 us
    dot_general x24, matrix products, contract_rows(): lax.dot_general(left, right, (((0,), (0,)), ((), ())), preferred_element_...  51.2 us
    psum x1, blocking collectives, per_device(): sums = lax.psum(one_axis, 'bal')  35.5 us
    psum x1, blocking collectives, per_device(): one_axis = lax.psum((terms[0], terms[1], terms[2], terms[3]), 'grp')  27.8 us
    another operation x1, loops' own time, pack_histories(): final_state, ranks = lax.scan(advance, start_state, seq_lengths)  20.9 us
  transfers between devices with their start and end apart: 5, of which 3 were waited for; matrix products, arithmetic and copies ran while one was open for 17% of the time, Pallas kernels for 0%

profile of v1, /device:TPU:1, one launch (start us, length us, event | category | flops | bytes accessed | tf_op | source)
XLA Modules:
  0.0 857.0 jit_solution(7507314394235276217)
XLA Ops:
  7.2 42.6 %while.66 = (s32[]{:T(128)}, s32[]{:T(128)}, s32[]{:T(128)}, s32[16]{0:T(128)S(1)}, s32[16]{0:T(128)}) while((s32[]{:T(128)}, s32[]{:T(128)}, s32[]{:T(128)}, s32[16]{0:T(128)S(1)}, s32[16]{0:T(128)}) %tuple.201), condition=%wide.region_3.4_spmd.clone, body=%wide.region_2.3_spmd.sunk.clone | while | flops 8 | bytes 148 | solution.py:137
  55.1 9.3 %all-to-all-start.1 = ((bf16[16,64,512]{2,1,0:T(8,128)(2,1)}), bf16[16,64,512]{2,1,0:T(8,128)(2,1)S(1)}, u32[]{:S(2)}, u32[]{:S(2)}) async-start(bf16[16,64,512]{2,1,0:T(8,128)(2,1)} %bitcast.70), calls=%async_computation.1 | async-start | bytes 2097152 | tf_op jit(solution)/shard_map/all_to_all | solution.py:248
  70.0 11.6 %all-to-all-done.1 = bf16[16,64,512]{2,1,0:T(8,128)(2,1)S(1)} async-done(((bf16[16,64,512]{2,1,0:T(8,128)(2,1)}), bf16[16,64,512]{2,1,0:T(8,128)(2,1)S(1)}, u32[]{:S(2)}, u32[]{:S(2)}) %all-to-all-start.1) | async-done | bytes 1048608 | tf_op jit(solution)/shard_map/all_to_all | solution.py:248
  81.6 5.0 all-to-all-start
  91.9 70.2 %while.67 = (s32[]{:T(128)}, f32[4,256,512]{2,1,0:T(8,128)}, f32[4,256,1]{1,2,0:T(1,128)}, bf16[4,256,512]{2,1,0:T(8,128)(2,1)}, f32[4,256,2048]{2,1,0:T(8,128)}...) while((s32[]{:T(128)}, f32[4,256,512]{2,1,0:T(8,128)}, ...), condition=%wide.region_16.17_spmd.clone, body=%wide.region_11.16_spmd.sunk.clone | while | flops 541589760 | bytes 17060060 | solution.py:152
  93.2 9.2 %conditional.9 = (f32[1,256,512]{2,1,0:T(8,128)S(1)}, f32[1,256,1]{1,2,0:T(1,128)}, bf16[1,256,512]{2,1,0:T(8,128)(2,1)S(1)}, f32[1,256,2048]{2,1,0:T(8,128)}, bf16[1,256,2048]{2,1,0:T(8,128)(2,1)S(1)}) conditional(s32[]{:T(128)} %convert_element_type.475, () %tuple.157, (bf16[4,256,512]{2,1,0:T(8,128)(2,1)}, s32[]{:T(128)}, f32[512]{0:T(512)S(1)}, ...), branch_computations={%region_12.12_spmd, %region_13.15_spmd} | conditional | flops 541589760 | bytes 9190964 | solution.py:150
  110.8 9.2 %conditional.9 = (f32[1,256,512]{2,1,0:T(8,128)S(1)}, f32[1,256,1]{1,2,0:T(1,128)}, bf16[1,256,512]{2,1,0:T(8,128)(2,1)S(1)}, f32[1,256,2048]{2,1,0:T(8,128)}, bf16[1,256,2048]{2,1,0:T(8,128)(2,1)S(1)}) conditional(s32[]{:T(128)} %convert_element_type.475, () %tuple.157, (bf16[4,256,512]{2,1,0:T(8,128)(2,1)}, s32[]{:T(128)}, f32[512]{0:T(512)S(1)}, ...), branch_computations={%region_12.12_spmd, %region_13.15_spmd} | conditional | flops 541589760 | bytes 9190964 | solution.py:150
  128.4 9.2 %conditional.9 = (f32[1,256,512]{2,1,0:T(8,128)S(1)}, f32[1,256,1]{1,2,0:T(1,128)}, bf16[1,256,512]{2,1,0:T(8,128)(2,1)S(1)}, f32[1,256,2048]{2,1,0:T(8,128)}, bf16[1,256,2048]{2,1,0:T(8,128)(2,1)S(1)}) conditional(s32[]{:T(128)} %convert_element_type.475, () %tuple.157, (bf16[4,256,512]{2,1,0:T(8,128)(2,1)}, s32[]{:T(128)}, f32[512]{0:T(512)S(1)}, ...), branch_computations={%region_12.12_spmd, %region_13.15_spmd} | conditional | flops 541589760 | bytes 9190964 | solution.py:150
  145.9 9.2 %conditional.9 = (f32[1,256,512]{2,1,0:T(8,128)S(1)}, f32[1,256,1]{1,2,0:T(1,128)}, bf16[1,256,512]{2,1,0:T(8,128)(2,1)S(1)}, f32[1,256,2048]{2,1,0:T(8,128)}, bf16[1,256,2048]{2,1,0:T(8,128)(2,1)S(1)}) conditional(s32[]{:T(128)} %convert_element_type.475, () %tuple.157, (bf16[4,256,512]{2,1,0:T(8,128)(2,1)}, s32[]{:T(128)}, f32[512]{0:T(512)S(1)}, ...), branch_computations={%region_12.12_spmd, %region_13.15_spmd} | conditional | flops 541589760 | bytes 9190964 | solution.py:150
  186.4 19.1 %select_convert_fusion.8 = (bf16[1024,1024]{1,0:T(8,128)(2,1)S(1)}, bf16[1024,1024]{1,0:T(8,128)(2,1)}, bf16[1024,1024]{1,0:T(8,128)(2,1)}, bf16[1024,1024]{1,0:...) fusion(pred[1024]{0:T(1024)(128)(4,1)S(1)} %broadcast_compare_f, ...), kind=kOutput, calls=%fused_computation.122 | convolution fusion | flops 197132288 | bytes 50865152 | tf_op jit(solution)/shard_map/dot_general | solution.py:40
  237.3 35.1 %while.68 = (s32[]{:T(128)}, f32[4,256,512]{2,1,0:T(8,128)}, bf16[4,256,512]{2,1,0:T(8,128)(2,1)}, f32[4,512,512]{2,1,0:T(8,128)}, f32[4,512]{1,0:T(4,128)S(1)},...) while((s32[]{:T(128)}, f32[4,256,512]{2,1,0:T(8,128)}, ...), condition=%wide.region_25.26_spmd.clone, body=%wide.region_17.25_spmd.sunk.clone | while | flops 273415936 | bytes 9736943 | solution.py:152
  282.7 5.2 select_convert_fusion.1
  288.0 4.9 select_convert_fusion.2
  307.4 4.9 select_convert_fusion.6
  317.2 4.9 select_convert_fusion
  372.0 5.6 pad_maximum_fusion
  377.8 67.9 %while.69 = (s32[]{:T(128)}, bf16[4,256,512]{2,1,0:T(8,128)(2,1)S(1)}, f32[4,512,2048]{2,1,0:T(8,128)}, f32[4,512]{1,0:T(4,128)S(1)}, s32[4]{0:T(128)S(1)}, /*in...) while((s32[]{:T(128)}, ...), condition=%wide.region_32.33_spmd.clone, body=%wide.region_26.32_spmd.sunk.clone | while | flops 1085013504 | bytes 26500880 | solution.py:152
  379.3 10.9 %conditional.11 = (bf16[1,256,512]{2,1,0:T(8,128)(2,1)S(1)}, f32[1,512,2048]{2,1,0:T(8,128)}, f32[1,512]{1,0:T(1,128)S(1)}) conditional(s32[]{:T(128)} %convert_element_type.477, () %tuple.167, (bf16[4,256,512]{2,1,0:T(8,128)(2,1)}, s32[]{:T(128)}, f32[4,256,1]{1,2,0:T(1,128)}, f32[4,256,2048]{2,1,0:T(8,128)}, f32[4,256,2048]{2,1,0:T(8,128)}, ...), branch_computations={%region_27.27_spmd, %region_28.31_spmd} | conditional | flops 1085013504 | bytes 17583136 | solution.py:150
  384.7 5.5 convolution_bitcast_fusion.1
  396.1 10.9 %conditional.11 = (bf16[1,256,512]{2,1,0:T(8,128)(2,1)S(1)}, f32[1,512,2048]{2,1,0:T(8,128)}, f32[1,512]{1,0:T(1,128)S(1)}) conditional(s32[]{:T(128)} %convert_element_type.477, () %tuple.167, (bf16[4,256,512]{2,1,0:T(8,128)(2,1)}, s32[]{:T(128)}, f32[4,256,1]{1,2,0:T(1,128)}, f32[4,256,2048]{2,1,0:T(8,128)}, f32[4,256,2048]{2,1,0:T(8,128)}, ...), branch_computations={%region_27.27_spmd, %region_28.31_spmd} | conditional | flops 1085013504 | bytes 17583136 | solution.py:150
  401.6 5.5 convolution_bitcast_fusion.1
  413.1 11.0 %conditional.11 = (bf16[1,256,512]{2,1,0:T(8,128)(2,1)S(1)}, f32[1,512,2048]{2,1,0:T(8,128)}, f32[1,512]{1,0:T(1,128)S(1)}) conditional(s32[]{:T(128)} %convert_element_type.477, () %tuple.167, (bf16[4,256,512]{2,1,0:T(8,128)(2,1)}, s32[]{:T(128)}, f32[4,256,1]{1,2,0:T(1,128)}, f32[4,256,2048]{2,1,0:T(8,128)}, f32[4,256,2048]{2,1,0:T(8,128)}, ...), branch_computations={%region_27.27_spmd, %region_28.31_spmd} | conditional | flops 1085013504 | bytes 17583136 | solution.py:150
  418.5 5.5 convolution_bitcast_fusion.1
  430.0 11.0 %conditional.11 = (bf16[1,256,512]{2,1,0:T(8,128)(2,1)S(1)}, f32[1,512,2048]{2,1,0:T(8,128)}, f32[1,512]{1,0:T(1,128)S(1)}) conditional(s32[]{:T(128)} %convert_element_type.477, () %tuple.167, (bf16[4,256,512]{2,1,0:T(8,128)(2,1)}, s32[]{:T(128)}, f32[4,256,1]{1,2,0:T(1,128)}, f32[4,256,2048]{2,1,0:T(8,128)}, f32[4,256,2048]{2,1,0:T(8,128)}, ...), branch_computations={%region_27.27_spmd, %region_28.31_spmd} | conditional | flops 1085013504 | bytes 17583136 | solution.py:150
  435.5 5.5 convolution_bitcast_fusion.1
  445.7 10.1 %reduce_sum.224 = f32[512,2048]{1,0:T(8,128)} reduce(f32[4,512,2048]{2,1,0:T(8,128)} %get-tuple-element.445, f32[]{:T(128)} %constant.270.clone.1), dimensions={0}, to_apply=%region_33.34 | reduce | flops 3145728 | bytes 20971524 | tf_op jit(solution)/shard_map/reduce_sum | solution.py:199
  459.6 221.8 %all-reduce.9.cloned.1.call-done = (f32[512,2048]{1,0:T(8,128)}, f32[512,512]{1,0:T(8,128)}) async-done(((f32[512,2048]{1,0:T(8,128)}, f32[512,512]{1,0:T(8,128)}), (f32[512,2048]{1,0:T(8,128)}, f32[512,512]{1,0:T(8,128)})) %all-reduce.9.cloned.1.call-update) | async-done | bytes 5242896 | tf_op jit(solution)/shard_map/psum | solution.py:272
  683.9 7.4 all-to-all-start.2
  691.4 27.8 %all-reduce.2 = (f32[512]{0:T(512)S(1)}, f32[512]{0:T(512)S(1)}) all-reduce(f32[512]{0:T(512)S(1)} %reduce_sum.226, f32[512]{0:T(512)S(1)} %reduce_sum.227), channel_id=1, replica_groups=mesh['grp'=8,'bal'=16] {'grp'}, use_global_device_ids=true, to_apply=%region_40.41 | all-reduce | flops 1024 | bytes 8192 | tf_op jit(solution)/shard_map/psum | solution.py:272
  719.2 35.5 %all-reduce = (f32[512]{0:T(512)S(1)}, f32[512]{0:T(512)S(1)}) all-reduce(f32[512]{0:T(512)S(1)} %get-tuple-element.559, f32[512]{0:T(512)S(1)} %get-tuple-element.560), channel_id=1, replica_groups=mesh['grp'=8,'bal'=16] {'bal'}, use_global_device_ids=true, to_apply=%region_41.42 | all-reduce | flops 1024 | bytes 8192 | tf_op jit(solution)/shard_map/psum | solution.py:273
  757.9 86.2 %all-reduce.7.cloned.1.call-done = (f32[512,2048]{1,0:T(8,128)}, f32[512,512]{1,0:T(8,128)}) async-done(((f32[512,2048]{1,0:T(8,128)}, f32[512,512]{1,0:T(8,128)}), (f32[512,2048]{1,0:T(8,128)}, f32[512,512]{1,0:T(8,128)})) %all-reduce.7.cloned.1.call-update) | async-done | bytes 5242896 | tf_op jit(solution)/shard_map/psum | solution.py:273
  844.0 4.9 broadcast_multiply_fusion.6
  (408 shorter events, 344.6 us)
Async XLA Ops:
  7.2 60.8 %copy-start.36 = (bf16[1,512,512]{2,1,0:T(8,128)(2,1)S(1)}, bf16[1,512,512]{2,1,0:T(8,128)(2,1)}, u32[]{:S(2)}) copy-start(bf16[1,512,512]{2,1,0:T(8,128)(2,1)} %param.22) | copy-start | bytes 1572868
  52.0 16.6 %copy-start.40 = (s32[8]{0:T(128)}, s32[8]{0:T(128)S(1)}, u32[]{:S(2)}) copy-start(s32[8]{0:T(128)S(1)} %fusion.169) | copy-start | bytes 100
  55.1 26.5 %all-to-all-start.1 = ((bf16[16,64,512]{2,1,0:T(8,128)(2,1)}), bf16[16,64,512]{2,1,0:T(8,128)(2,1)S(1)}, u32[]{:S(2)}, u32[]{:S(2)}) async-start(bf16[16,64,512]{2,1,0:T(8,128)(2,1)} %bitcast.70), calls=%async_computation.1 | async-start | bytes 2097152 | tf_op jit(solution)/shard_map/all_to_all | solution.py:248
  67.0 163.3 %copy-start.42 = (s32[16]{0:T(128)}, s32[16]{0:T(128)S(1)}, u32[]{:S(2)}) copy-start(s32[16]{0:T(128)S(1)} %get-tuple-element.582) | copy-start | bytes 196
  81.6 147.0 %all-to-all-start = ((bf16[16,64,512]{2,1,0:T(8,128)(2,1)}), bf16[16,64,512]{2,1,0:T(8,128)(2,1)}, u32[]{:S(2)}, u32[]{:S(2)}) async-start(bf16[16,64,512]{2,1,0:T(8,128)(2,1)} %bitcast.66), calls=%async_computation | async-start | bytes 2097152 | tf_op jit(solution)/shard_map/all_to_all | solution.py:251
  86.6 594.9 %all-reduce.9.cloned.1.call-start = ((), (), s32[]{:S(2)}) async-start(), calls=%async_computation.4 | async-start | bytes 10485760 | tf_op jit(solution)/shard_map/psum | solution.py:272
  186.4 19.1 %copy-start.15 = (f32[1024,1024]{1,0:T(8,128)}, f32[1024,1024]{1,0:T(8,128)S(1)}, u32[]{:S(2)}) copy-start(f32[1024,1024]{1,0:T(8,128)S(1)} %fusion.155) | copy-start | bytes 12582916
  205.5 7.7 copy-start.8
  205.5 7.7 copy-start.10
  205.5 7.7 copy-start.6
  205.5 9.4 %copy-start.12 = (bf16[1024,1024]{1,0:T(8,128)(2,1)}, bf16[1024,1024]{1,0:T(8,128)(2,1)S(1)}, u32[]{:S(2)}) copy-start(bf16[1024,1024]{1,0:T(8,128)(2,1)S(1)} %get-tuple-element.579) | copy-start | bytes 6291460
  205.5 9.4 %copy-start.13 = (bf16[1024,1024]{1,0:T(8,128)(2,1)}, bf16[1024,1024]{1,0:T(8,128)(2,1)S(1)}, u32[]{:S(2)}) copy-start(bf16[1024,1024]{1,0:T(8,128)(2,1)S(1)} %get-tuple-element.573) | copy-start | bytes 6291460
  205.5 20.4 %copy-start.2 = (bf16[1024,1024]{1,0:T(8,128)(2,1)}, bf16[1024,1024]{1,0:T(8,128)(2,1)S(1)}, u32[]{:S(2)}) copy-start(bf16[1024,1024]{1,0:T(8,128)(2,1)S(1)} %get-tuple-element.580) | copy-start | bytes 6291460
  230.8 6.4 copy-start.37
  272.4 5.3 copy-start.38
  282.7 5.2 copy-start.21
  288.0 4.9 copy-start.20
  297.7 4.9 copy-start.18
  307.4 4.9 copy-start.16
  312.3 4.8 copy-start.44
  359.1 4.9 copy-start.32
  359.1 5.1 copy-start.33
  359.1 5.2 copy-start.34
  359.1 5.4 copy-start.35
  372.0 5.8 copy-start.1
  372.0 5.8 copy-start.31
  459.6 222.5 %copy-start.43 = (s32[16]{0:T(128)S(1)}, s32[16]{0:T(128)}, u32[]{:S(2)}) copy-start(s32[16]{0:T(128)} %copy-done.42) | copy-start | bytes 196
  459.6 384.4 %all-reduce.7.cloned.1.call-start = ((), (), s32[]{:S(2)}) async-start(), calls=%async_computation.3 | async-start | bytes 10485760 | tf_op jit(solution)/shard_map/psum | solution.py:273
  681.5 9.9 %copy-start.39 = (f32[4,512]{1,0:T(4,128)S(1)}, f32[4,512]{1,0:T(4,128)}, u32[]{:S(2)}) copy-start(f32[4,512]{1,0:T(4,128)} %copy-done.38) | copy-start | bytes 24580
  682.0 74.4 %copy-start.41 = (s32[8]{0:T(128)S(1)}, s32[8]{0:T(128)}, u32[]{:S(2)}) copy-start(s32[8]{0:T(128)} %copy-done.40) | copy-start | bytes 100
  683.9 72.0 %all-to-all-start.2 = ((bf16[16,64,512]{2,1,0:T(8,128)(2,1)}), bf16[16,64,512]{2,1,0:T(8,128)(2,1)S(1)}, u32[]{:S(2)}, u32[]{:S(2)}) async-start(bf16[16,64,512]{2,1,0:T(8,128)(2,1)} %bitcast.74), calls=%async_computation.2 | async-start | bytes 2097152 | tf_op jit(solution)/shard_map/all_to_all | solution.py:268
  844.0 4.9 copy-start.25
  (18 other events, 57.2 us)
Sparse Core Ops, SparseCore 0:
  459.7 221.7 all-reduce.8
  684.0 159.9 all-reduce.6
